TPU v7x, 32 devices: a whole 2x2x4 slice. The times are simulated.
32 devices in a mesh: section: 4 (over y, core), chan: 8 (over z, x).
Axes of the slice: x: 2, y: 2, z: 4, core: 2. Of those that a mesh axis runs over, the one named last changes fastest.
Arguments:
- raw_traces: bfloat16 [2048, 1024], P(('section', 'chan')), may hold values from -6 to 6
- fir_taps: bfloat16 [64], replicated, may hold values from -0.75 to 0.75
- space_taps: float32 [33], replicated, may hold values from -1 to 1
- source_index: int32 [4, 96], P('section', 'chan'), may hold values from 0 to 511, as said below
Outputs:
- gathers: bfloat16 [2048, 64, 96], P(('section', 'chan'))
Inputs may be any that keep to these rules, and one draw needn't show every extreme that they name: `source_index`: entries j * 12 to (j + 1) * 12 - 1 of a section's row are distinct and lie in channels j * 64 to (j + 1) * 64 - 1; the first such block of every section names channel 0 and the last names channel 512 - 1.
All inputs are finite; a program needn't handle non-finite values.
Results may differ from a plain program's by a relative error of at most 0.0058.
Values may be sent and summed in bfloat16 or wider, within the bound.
A program may use at most 64 MiB of HBM per device.

v0:
```python
import jax
import jax.numpy as jnp
from jax import lax
from jax.sharding import PartitionSpec as P

LAGS = 64


def extended(x, sides, width):
    for axis, dim in sides:
        size, length = (lax.axis_size(axis), x.shape[dim])
        up = [(i, (i + 1) % size) for i in range(size - 1)]
        down = [(j, i) for i, j in up]
        last = lax.slice_in_dim(x, length - width, length, axis=dim)
        leading = lax.slice_in_dim(x, 0, width, axis=dim)
        before = lax.ppermute(last, axis, up)
        after = lax.ppermute(leading, axis, down)
        x = jnp.concatenate([before, x, after], axis=dim)
    return x


def fir_matrix(taps, length):
    count = taps.shape[0]
    lead = jnp.zeros((length - 1,), taps.dtype)
    tail = jnp.zeros((length + 1 - count,), taps.dtype)
    period = jnp.concatenate([lead, taps, tail])
    flat = jnp.tile(period, length)[: length * (2 * length - 1)]
    return flat.reshape(length, 2 * length - 1)[:, length - 1 :]


def space_filter(padded, space_taps, rows):
    total = jnp.zeros((rows, padded.shape[1]), jnp.float32)
    for offset in range(space_taps.shape[0]):
        total = total + space_taps[offset] * padded[offset : offset + rows].astype(jnp.float32)
    return total.astype(jnp.bfloat16)


def correlate(receivers, sources):
    rows, length = receivers.shape
    blocks = []
    for first in range(0, LAGS, 8):
        shifted = []
        for lag in range(first, first + 8):
            shifted.append(jnp.pad(receivers[:, lag:], ((0, 0), (0, lag))))
        stacked = jnp.stack(shifted, axis=1).reshape(rows * 8, length)
        block = lax.dot_general(
            stacked, sources, (((1,), (1,)), ((), ())), preferred_element_type=jnp.float32
        )
        blocks.append(block.reshape(rows, 8, sources.shape[0]))
    joined = jnp.concatenate(blocks, axis=1)
    return (joined * (1.0 / length**0.5)).astype(jnp.bfloat16)


def shards(raw_traces, fir_taps, space_taps, source_index):
    rows, length = raw_traces.shape
    banded = jnp.dot(
        raw_traces, fir_matrix(fir_taps, length), preferred_element_type=jnp.float32
    ).astype(jnp.bfloat16)
    half = (space_taps.shape[0] - 1) // 2
    padded = extended(banded, ((("section", "chan"), 0),), half)
    filtered = space_filter(padded, space_taps, rows)
    whole_traces, whole_index = (
        lax.all_gather(filtered, "chan", axis=0, tiled=True),
        lax.all_gather(source_index, "chan", axis=1, tiled=True),
    )
    sources = jnp.take(whole_traces, whole_index[0], axis=0)
    return correlate(filtered, sources)


def solution(mesh):
    return jax.shard_map(
        shards,
        mesh=mesh,
        in_specs=(P(("section", "chan"), None), P(), P(), P("section", "chan")),
        out_specs=P(("section", "chan"), None, None),
        check_vma=False,
    )
```

profile of v0, /device:TPU:0, one launch (start us, length us, event | category | flops | bytes accessed | tf_op | source)
XLA Modules:
  0.0 132.3 jit_solution(16714103273075158136)
XLA Ops:
  6.5 0.8 concatenate.43
  7.3 1.0 broadcast_bitcast_fusion
  8.4 1.4 %copy.29 = bf16[128,16,8,128]{3,1,2,0:T(8,128)(2,1)S(1)} copy(bf16[128,16,8,128]{3,2,1,0:T(8,128)(2,1)S(1)} %broadcast_bitcast_fusion) | data formatting | bytes 8388608
  9.8 2.2 %slice.562 = bf16[2096128]{0:T(1024)(128)(2,1)} slice(bf16[2097152]{0:T(1024)(128)(2,1)S(1)} %bitcast.199), slice={[0:2096128]} | slice | bytes 8384512 | tf_op jit(solution)/shard_map/slice | solution.py:27
  12.0 10.7 %reshape.70 = bf16[1024,2047]{1,0:T(8,128)(2,1)} reshape(bf16[2096128]{0:T(1024)(128)(2,1)} %slice.562) | data formatting | bytes 8384512 | tf_op jit(solution)/shard_map/reshape | solution.py:28
  22.7 2.5 %fusion.5 = bf16[64,1024]{1,0:T(8,128)(2,1)S(1)} fusion(bf16[64,1024]{1,0:T(8,128)(2,1)S(1)} %copy-done, bf16[1024,2047]{1,0:T(8,128)(2,1)} %reshape.70), kind=kOutput, calls=%fused_computation.6 | convolution fusion | flops 134283264 | bytes 2359296 | tf_op jit(solution)/shard_map/dot_general | solution.py:56
  25.2 1.3 collective-permute-start.1
  26.5 5.5 %collective-permute-start = (bf16[16,1024]{1,0:T(8,128)(2,1)S(1)}, bf16[16,1024]{1,0:T(8,128)(2,1)S(1)}, u32[]{:S(2)}, u32[]{:S(2)}) collective-permute-start(bf16[16,1024]{1,0:T(8,128)(2,1)S(1)} %get-tuple-element.7), channel_id=1, source_target_pairs={{0,1},{1,2},{2,3},{3,4},{4,5},{5,6},{6,7},{7,8},{8,9},{9,10},{10,1... | collective-permute-start | bytes 98312 | tf_op jit(solution)/shard_map/ppermute | solution.py:16
  32.0 0.7 fusion.57
  32.7 0.7 fusion.56
  33.5 0.6 dynamic-slice
  34.7 14.0 %all-reduce.63 = s32[96]{0:T(128)S(1)} all-reduce(s32[96]{0:T(128)S(1)} %bitcast_dynamic-update-slice_fusion), channel_id=1, replica_groups=mesh['section'=4,'chan'=8] {'chan'}, use_global_device_ids=true, to_apply=%add.63 | all-reduce | flops 96 | bytes 768 | tf_op jit(solution)/shard_map/squeeze | solution.py:66
  48.8 21.9 %constant_dynamic-update-slice_fusion.7 = (bf16[64,8,1024]{2,0,1:T(8,128)(2,1)S(1)}, bf16[64,1024]{1,0:T(8,128)(2,1)S(1)}) fusion(bf16[16,1024]{1,0:T(8,128)(2,1)S(1)} %collective-permute-done.1, bf16[64,1024]{1,0:T(8,128)(2,1)S(1)} %fusion.5, f32[]{:T(128)} %bitcast.33, f32[]{:T(128)} %bitcast.32, f32[]{:T(128)} %bitcast.31, f32[]{:T(128)} %bitcast.30, ...), kind=kLoop, calls=%fused_computation.70 | loop fusion | flops 12779519 | bytes 458884
  70.7 0.8 slice.626
  71.5 0.8 slice.627
  72.2 0.8 slice.628
  73.0 0.8 slice.629
  73.7 0.8 slice.630
  74.5 0.8 slice.631
  75.3 0.8 slice.632
  76.1 1.1 slice.633
  77.1 1.0 slice.634
  78.2 1.0 slice.635
  79.2 1.0 slice.636
  80.2 1.0 slice.637
  81.2 1.0 slice.638
  82.2 1.0 slice.639
  83.2 1.0 slice.640
  90.8 0.6 copy-done.11
  91.6 0.2 copy-done.9
  91.9 0.2 copy-done.7
  92.3 0.2 copy-done.5
  92.6 0.3 copy-done.3
  92.9 22.2 %all-gather.2.cloned.1.call-done = bf16[512,1024]{1,0:T(8,128)(2,1)} async-done(((bf16[64,1024]{1,0:T(8,128)(2,1)}), bf16[512,1024]{1,0:T(8,128)(2,1)}) %all-gather.2.cloned.1.call-update) | async-done | bytes 1048592 | tf_op jit(solution)/shard_map/all_gather | solution.py:63
  115.1 2.3 %gather_fusion = bf16[96,1024]{1,0:T(8,128)(2,1)S(1)} fusion(bf16[512,1024]{1,0:T(8,128)(2,1)} %all-gather.2.cloned.1.call-done, s32[1024]{0:T(1024)S(1)} %pad_clamp_fusion), kind=kCustom, calls=%fused_computation | custom fusion | bytes 393600 | tf_op jit(solution)/shard_map/jit(_take)/gather | solution.py:66
  117.4 0.5 fusion.22
  118.1 1.8 %fusion.20 = f32[64,8,96]{2,0,1:T(8,128)S(1)} fusion(bf16[64,8,1024]{2,0,1:T(8,128)(2,1)} %copy-done.11, bf16[96,1024]{1,0:T(8,128)(2,1)S(1)} %gather_fusion, pred[96]{0:T(512)(128)(4,1)S(1)} %compare_and_fusion), kind=kOutput, calls=%fused_computation.58 | convolution fusion | flops 100761600 | bytes 1441888 | tf_op jit(solution)/shard_map/dot_general | solution.py:46
  120.0 0.5 fusion.18
  120.5 0.5 fusion.16
  121.0 0.5 fusion.14
  121.5 0.5 fusion.12
  122.0 0.5 fusion.10
  122.6 0.5 fusion.8
  123.1 0.2 copy_dynamic-update-slice_fusion.6
  123.2 0.2 copy_dynamic-update-slice_fusion.5
  123.6 0.2 copy_dynamic-update-slice_fusion.3
  123.7 0.2 copy_dynamic-update-slice_fusion.2
  124.2 1.2 multiply_convert_fusion
  (166 shorter events, 7.1 us)
Async XLA Ops:
  6.5 16.1 %copy-start = (bf16[64,1024]{1,0:T(8,128)(2,1)S(1)}, bf16[64,1024]{1,0:T(8,128)(2,1)}, u32[]{:S(2)}) copy-start(bf16[64,1024]{1,0:T(8,128)(2,1)} %param.4) | copy-start | bytes 393220
  6.5 108.6 %all-gather.2.cloned.1.call-start = ((), (), s32[]{:S(2)}) async-start(), calls=%async_computation | async-start | bytes 1179648 | tf_op jit(solution)/shard_map/all_gather | solution.py:63
  22.7 9.3 %copy-start.12 = (f32[33]{0:T(128)S(1)}, f32[33]{0:T(128)}, u32[]{:S(2)}) copy-start(f32[33]{0:T(128)} %param.6) | copy-start | bytes 400
  22.7 10.8 %copy-start.21 = (u32[32]{0:T(128)S(1)}, u32[32]{0:T(128)}, u32[]{:S(2)}) copy-start(u32[32]{0:T(128)} %constant.152) | copy-start | bytes 388
  22.7 11.9 %copy-start.20 = (s32[1,12]{1,0:T(1,128)S(1)}, s32[1,12]{1,0:T(1,128)}, u32[]{:S(2)}) copy-start(s32[1,12]{1,0:T(1,128)} %param.7) | copy-start | bytes 148
  25.2 23.5 %collective-permute-start.1 = (bf16[16,1024]{1,0:T(8,128)(2,1)S(1)}, bf16[16,1024]{1,0:T(8,128)(2,1)S(1)}, u32[]{:S(2)}, u32[]{:S(2)}) collective-permute-start(bf16[16,1024]{1,0:T(8,128)(2,1)S(1)} %get-tuple-element.8), channel_id=1, source_target_pairs={{1,0},{2,1},{3,2},{4,3},{5,4},{6,5},{7,6},{8,7},{9,8},{10,9},{11,1... | collective-permute-start | bytes 98312 | tf_op jit(solution)/shard_map/ppermute | solution.py:17
  26.5 22.2 %collective-permute-start = (bf16[16,1024]{1,0:T(8,128)(2,1)S(1)}, bf16[16,1024]{1,0:T(8,128)(2,1)S(1)}, u32[]{:S(2)}, u32[]{:S(2)}) collective-permute-start(bf16[16,1024]{1,0:T(8,128)(2,1)S(1)} %get-tuple-element.7), channel_id=1, source_target_pairs={{0,1},{1,2},{2,3},{3,4},{4,5},{5,6},{6,7},{7,8},{8,9},{9,10},{10,1... | collective-permute-start | bytes 98312 | tf_op jit(solution)/shard_map/ppermute | solution.py:16
  70.7 5.3 %copy-start.1 = (bf16[64,1024]{1,0:T(8,128)(2,1)}, bf16[64,1024]{1,0:T(8,128)(2,1)S(1)}, u32[]{:S(2)}) copy-start(bf16[64,1024]{1,0:T(8,128)(2,1)S(1)} %get-tuple-element.6) | copy-start | bytes 393220
  76.1 8.2 %copy-start.2 = (bf16[64,1024]{1,0:T(8,128)(2,1)S(1)}, bf16[64,1024]{1,0:T(8,128)(2,1)}, u32[]{:S(2)}) copy-start(bf16[64,1024]{1,0:T(8,128)(2,1)} %copy-done.1) | copy-start | bytes 393220
  88.6 1.2 copy-start.19
  88.7 1.1 copy-start.18
  88.8 1.0 copy-start.17
  88.9 1.0 copy-start.16
  89.1 1.0 copy-start.15
  89.2 1.0 copy-start.14
  89.3 1.0 copy-start.13
  90.4 1.0 copy-start.11
  90.6 1.1 copy-start.9
  90.8 1.4 %copy-start.7 = (bf16[64,8,1024]{2,0,1:T(8,128)(2,1)}, bf16[64,8,1024]{2,0,1:T(8,128)(2,1)S(1)}, u32[]{:S(2)}) copy-start(bf16[64,8,1024]{2,0,1:T(8,128)(2,1)S(1)} %constant_dynamic-update-slice_fusion.24) | copy-start | bytes 3145732
  91.5 1.0 copy-start.5
  91.9 1.0 copy-start.3
  117.4 2.5 %copy-start.10 = (bf16[64,8,1024]{2,0,1:T(8,128)(2,1)S(1)}, bf16[64,8,1024]{2,0,1:T(8,128)(2,1)}, u32[]{:S(2)}) copy-start(bf16[64,8,1024]{2,0,1:T(8,128)(2,1)} %copy-done.9) | copy-start | bytes 3145732
  117.9 2.6 %copy-start.8 = (bf16[64,8,1024]{2,0,1:T(8,128)(2,1)S(1)}, bf16[64,8,1024]{2,0,1:T(8,128)(2,1)}, u32[]{:S(2)}) copy-start(bf16[64,8,1024]{2,0,1:T(8,128)(2,1)} %copy-done.7) | copy-start | bytes 3145732
  118.1 2.9 %copy-start.6 = (bf16[64,8,1024]{2,0,1:T(8,128)(2,1)S(1)}, bf16[64,8,1024]{2,0,1:T(8,128)(2,1)}, u32[]{:S(2)}) copy-start(bf16[64,8,1024]{2,0,1:T(8,128)(2,1)} %copy-done.5) | copy-start | bytes 3145732
  120.0 1.6 %copy-start.4 = (bf16[64,8,1024]{2,0,1:T(8,128)(2,1)S(1)}, bf16[64,8,1024]{2,0,1:T(8,128)(2,1)}, u32[]{:S(2)}) copy-start(bf16[64,8,1024]{2,0,1:T(8,128)(2,1)} %copy-done.3) | copy-start | bytes 3145732
Sparse Core Ops, SparseCore 0:
  76.2 38.9 all-gather.1
where the time goes:
time: 133 us; the launch traced here: 132 us
  local copies, waits for them, and re-layouts  43 us (32%)
  other arithmetic  23.2 us (17%)
  waiting for transfers between devices  22.3 us (17%)
  between operations  15.2 us (11%)
  blocking collectives  14 us (11%)
  matrix products  7.9 us (6%)
  starting transfers between devices  6.77 us (5%)
    all_gather x1, waiting for transfers between devices, shards(): lax.all_gather(filtered, 'chan', axis=0, tiled=True)  22.2 us
    unnamed x1, other arithmetic  21.9 us
    slice x63, local copies, waits for them, and re-layouts, correlate(): shifted.append(jnp.pad(receivers[:, lag:], ((0, 0), (0, lag))))  18.4 us
    squeeze x1, blocking collectives, shards(): sources = jnp.take(whole_traces, whole_index[0], axis=0)  14 us
    reshape x1, local copies, waits for them, and re-layouts, fir_matrix(): return flat.reshape(length, 2 * length - 1)[:, length - 1:]  10.7 us
    unnamed x111, local copies, waits for them, and re-layouts  6.9 us
    ppermute x1, starting transfers between devices, extended(): before = lax.ppermute(last, axis, up)  5.47 us
    dot_general x8, matrix products, correlate(): lax.dot_general(stacked, sources, (((1,), (1,)), ((), ())), preferred_ele...  5.37 us
  transfers between devices with their start and end apart: 3, of which 1 were waited for; matrix products, arithmetic and copies ran while one was open for 12% of the time, Pallas kernels for 0%

commit v1 on v0

--- a/solution.py
+++ b/solution.py
@@ -4,6 +4,28 @@
 from jax.sharding import PartitionSpec as P
 
 LAGS = 64
+
+
+def in_order(blocks, dim):
+    blocks = jnp.moveaxis(blocks, 0, dim)
+    lengths = blocks.shape
+    return blocks.reshape(*lengths[:dim], lengths[dim] * lengths[dim + 1], *lengths[dim + 2 :])
+
+
+def ring_gather(x, axis, dim):
+    size = lax.axis_size(axis)
+    pairs = [(i, (i + 1) % size) for i in range(size)]
+    back = [(b, a) for a, b in pairs]
+    lower, upper = ([], [])
+    for step in range(size - 1):
+        if step % 2 == 0:
+            lower.append(lax.ppermute(lower[-1] if lower else x, axis, pairs))
+        else:
+            upper.append(lax.ppermute(upper[-1] if upper else x, axis, back))
+    blocks = jnp.stack([*lower[::-1], x, *upper])
+    shift = lax.axis_index(axis) - len(lower)
+    blocks = blocks[(jnp.arange(size) - shift) % size]
+    return in_order(blocks, dim)
 
 
 def extended(x, sides, width):
@@ -60,7 +82,7 @@
     padded = extended(banded, ((("section", "chan"), 0),), half)
     filtered = space_filter(padded, space_taps, rows)
     whole_traces, whole_index = (
-        lax.all_gather(filtered, "chan", axis=0, tiled=True),
+        ring_gather(filtered, "chan", 0),
         lax.all_gather(source_index, "chan", axis=1, tiled=True),
     )
     sources = jnp.take(whole_traces, whole_index[0], axis=0)

time: 133 us -> 111 us (0.83)
  starting transfers between devices: 6.77 us -> 21.3 us
  local copies, waits for them, and re-layouts: 43 us -> 29.5 us
  between operations: 15.2 us -> 2.09 us
  waiting for transfers between devices: 22.3 us -> 12.9 us
    all_gather x1 -> x0, waiting for transfers between devices: 22.2 us -> none  [shards(): lax.all_gather(filtered, 'chan', axis=0, tiled=True)]
    ppermute x0 -> x7, starting transfers between devices: none -> 14.5 us  [the longest x3 11.1 us: ring_gather(): upper.append(lax.ppermute(upper[-1] if upper else x, axis, back))]
    ppermute x0 -> x7, waiting for transfers between devices: none -> 12.9 us  [the longest x4 12.9 us: ring_gather(): lower.append(lax.ppermute(lower[-1] if lower else x, axis, pairs))]
    slice x63, local copies, waits for them, and re-layouts: 18.4 us -> 6.53 us  [correlate(): shifted.append(jnp.pad(receivers[:, lag:], ((0, 0), (0, lag))))]
    gather x1, local copies, waits for them, and re-layouts: 2.28 us -> 0.78 us  [shards(): sources = jnp.take(whole_traces, whole_index[0], axis=0)]
    unnamed x111 -> x108, local copies, waits for them, and re-layouts: 6.9 us -> 6.22 us
  transfers between devices with their start and end apart: 3 -> 9, of which waited for: 1 -> 3; matrix products, arithmetic and copies ran while one was open for 12% -> 8% of each run, Pallas kernels for 0% -> 0%
where the time goes in v1:
time: 111 us
  local copies, waits for them, and re-layouts  29.5 us (27%)
  other arithmetic  23.2 us (21%)
  starting transfers between devices  21.3 us (19%)
  blocking collectives  14 us (13%)
  waiting for transfers between devices  12.9 us (12%)
  matrix products  7.89 us (7%)
  between operations  2.09 us (2%)
    unnamed x1, other arithmetic  21.9 us
    squeeze x1, blocking collectives, shards(): sources = jnp.take(whole_traces, whole_index[0], axis=0)  14 us
    ppermute x4, waiting for transfers between devices, ring_gather(): lower.append(lax.ppermute(lower[-1] if lower else x, axis, pairs))  12.9 us
    ppermute x3, starting transfers between devices, ring_gather(): upper.append(lax.ppermute(upper[-1] if upper else x, axis, back))  11.1 us
    reshape x1, local copies, waits for them, and re-layouts, fir_matrix(): return flat.reshape(length, 2 * length - 1)[:, length - 1:]  10.7 us
    slice x63, local copies, waits for them, and re-layouts, correlate(): shifted.append(jnp.pad(receivers[:, lag:], ((0, 0), (0, lag))))  6.53 us
    unnamed x108, local copies, waits for them, and re-layouts  6.22 us
    ppermute x1, starting transfers between devices, extended(): before = lax.ppermute(last, axis, up)  5.48 us
  transfers between devices with their start and end apart: 9, of which 3 were waited for; matrix products, arithmetic and copies ran while one was open for 8% of the time, Pallas kernels for 0%

profile of v1, /device:TPU:0, one launch (start us, length us, event | category | flops | bytes accessed | tf_op | source)
XLA Modules:
  0.0 110.9 jit_solution(5490845186028973970)
XLA Ops:
  0.0 0.8 concatenate.43
  0.8 1.0 broadcast_bitcast_fusion
  1.8 1.4 %copy.29 = bf16[128,16,8,128]{3,1,2,0:T(8,128)(2,1)S(1)} copy(bf16[128,16,8,128]{3,2,1,0:T(8,128)(2,1)S(1)} %broadcast_bitcast_fusion) | data formatting | bytes 8388608
  3.3 2.2 %slice.564 = bf16[2096128]{0:T(1024)(128)(2,1)} slice(bf16[2097152]{0:T(1024)(128)(2,1)S(1)} %bitcast.218), slice={[0:2096128]} | slice | bytes 8384512 | tf_op jit(solution)/shard_map/slice | solution.py:49
  5.4 10.7 %reshape.122 = bf16[1024,2047]{1,0:T(8,128)(2,1)} reshape(bf16[2096128]{0:T(1024)(128)(2,1)} %slice.564) | data formatting | bytes 8384512 | tf_op jit(solution)/shard_map/reshape | solution.py:50
  16.1 2.5 %fusion.5 = bf16[64,1024]{1,0:T(8,128)(2,1)S(1)} fusion(bf16[64,1024]{1,0:T(8,128)(2,1)S(1)} %copy-done, bf16[1024,2047]{1,0:T(8,128)(2,1)} %reshape.122), kind=kOutput, calls=%fused_computation.7 | convolution fusion | flops 134283264 | bytes 2359296 | tf_op jit(solution)/shard_map/dot_general | solution.py:78
  18.7 1.3 %collective-permute-start.1 = (bf16[16,1024]{1,0:T(8,128)(2,1)S(1)}, bf16[16,1024]{1,0:T(8,128)(2,1)S(1)}, u32[]{:S(2)}, u32[]{:S(2)}) collective-permute-start(bf16[16,1024]{1,0:T(8,128)(2,1)S(1)} %get-tuple-element.8), channel_id=1, source_target_pairs={{1,0},{2,1},{3,2},{4,3},{5,4},{6,5},{7,6},{8,7},{9,8},{10,9},{11,1... | collective-permute-start | bytes 98312 | tf_op jit(solution)/shard_map/ppermute | solution.py:39
  20.0 5.5 %collective-permute-start = (bf16[16,1024]{1,0:T(8,128)(2,1)S(1)}, bf16[16,1024]{1,0:T(8,128)(2,1)S(1)}, u32[]{:S(2)}, u32[]{:S(2)}) collective-permute-start(bf16[16,1024]{1,0:T(8,128)(2,1)S(1)} %get-tuple-element.7), channel_id=1, source_target_pairs={{0,1},{1,2},{2,3},{3,4},{4,5},{5,6},{6,7},{7,8},{8,9},{9,10},{10,1... | collective-permute-start | bytes 98312 | tf_op jit(solution)/shard_map/ppermute | solution.py:38
  25.5 0.7 fusion.59
  26.2 0.7 fusion.58
  26.9 0.6 dynamic-slice
  28.4 14.0 %all-reduce.63 = s32[96]{0:T(128)S(1)} all-reduce(s32[96]{0:T(128)S(1)} %bitcast_dynamic-update-slice_fusion), channel_id=1, replica_groups=mesh['section'=4,'chan'=8] {'chan'}, use_global_device_ids=true, to_apply=%add.63 | all-reduce | flops 96 | bytes 768 | tf_op jit(solution)/shard_map/squeeze | solution.py:88
  42.5 21.9 %constant_dynamic-update-slice_fusion.7 = (bf16[64,8,1024]{2,0,1:T(8,128)(2,1)S(1)}, bf16[64,1024]{1,0:T(8,128)(2,1)S(1)}) fusion(bf16[16,1024]{1,0:T(8,128)(2,1)S(1)} %collective-permute-done.1, bf16[64,1024]{1,0:T(8,128)(2,1)S(1)} %fusion.5, f32[]{:T(128)} %bitcast.33, f32[]{:T(128)} %bitcast.32, f32[]{:T(128)} %bitcast.31, f32[]{:T(128)} %bitcast.30, ...), kind=kLoop, calls=%fused_computation.71 | loop fusion | flops 12779519 | bytes 458884
  65.0 0.1 slice.633
  65.2 2.1 %collective-permute-start.2 = (bf16[64,1024]{1,0:T(8,128)(2,1)S(1)}, bf16[64,1024]{1,0:T(8,128)(2,1)S(1)}, u32[]{:S(2)}, u32[]{:S(2)}) collective-permute-start(bf16[64,1024]{1,0:T(8,128)(2,1)S(1)} %get-tuple-element.6), channel_id=1, source_target_pairs={{0,1},{1,2},{2,3},{3,4},{4,5},{5,6},{6,7},{7,0},{8,9},{9,10},{10,1... | collective-permute-start | bytes 393224 | tf_op jit(solution)/shard_map/ppermute | solution.py:22
  67.3 2.7 %collective-permute-start.6 = (bf16[64,1024]{1,0:T(8,128)(2,1)S(1)}, bf16[64,1024]{1,0:T(8,128)(2,1)S(1)}, u32[]{:S(2)}, u32[]{:S(2)}) collective-permute-start(bf16[64,1024]{1,0:T(8,128)(2,1)S(1)} %get-tuple-element.6), channel_id=1, source_target_pairs={{1,0},{2,1},{3,2},{4,3},{5,4},{6,5},{7,6},{0,7},{9,8},{10,9},{11,1... | collective-permute-start | bytes 393224 | tf_op jit(solution)/shard_map/ppermute | solution.py:24
  70.6 0.1 slice.641
  71.0 0.1 slice.644
  71.3 0.1 slice.647
  71.6 0.1 slice.650
  76.2 0.6 copy-done.13
  77.0 0.2 copy-done.11
  77.3 0.1 copy-done.9
  78.2 7.4 %collective-permute-done.3 = bf16[64,1024]{1,0:T(8,128)(2,1)S(1)} collective-permute-done((bf16[64,1024]{1,0:T(8,128)(2,1)S(1)}, bf16[64,1024]{1,0:T(8,128)(2,1)S(1)}, u32[]{:S(2)}, u32[]{:S(2)}) %collective-permute-start.3) | collective-permute-done | bytes 131104 | tf_op jit(solution)/shard_map/ppermute | solution.py:22
  85.9 4.8 %collective-permute-start.7 = (bf16[64,1024]{1,0:T(8,128)(2,1)S(1)}, bf16[64,1024]{1,0:T(8,128)(2,1)S(1)}, u32[]{:S(2)}, u32[]{:S(2)}) collective-permute-start(bf16[64,1024]{1,0:T(8,128)(2,1)S(1)} %collective-permute-done.6), channel_id=1, source_target_pairs={{1,0},{2,1},{3,2},{4,3},{5,4},{6,5},{7,6},{0,7},{9,8},{10,9},{11,1... | collective-permute-start | bytes 393224 | tf_op jit(solution)/shard_map/ppermute | solution.py:24
  90.7 2.7 %collective-permute-done.4 = bf16[64,1024]{1,0:T(8,128)(2,1)S(1)} collective-permute-done((bf16[64,1024]{1,0:T(8,128)(2,1)S(1)}, bf16[64,1024]{1,0:T(8,128)(2,1)S(1)}, u32[]{:S(2)}, u32[]{:S(2)}) %collective-permute-start.4) | collective-permute-done | bytes 131104 | tf_op jit(solution)/shard_map/ppermute | solution.py:22
  93.4 1.3 %collective-permute-start.5 = (bf16[64,1024]{1,0:T(8,128)(2,1)S(1)}, bf16[64,1024]{1,0:T(8,128)(2,1)S(1)}, u32[]{:S(2)}, u32[]{:S(2)}) collective-permute-start(bf16[64,1024]{1,0:T(8,128)(2,1)S(1)} %collective-permute-done.4), channel_id=1, source_target_pairs={{0,1},{1,2},{2,3},{3,4},{4,5},{5,6},{6,7},{7,0},{8,9},{9,10},{10,1... | collective-permute-start | bytes 393224 | tf_op jit(solution)/shard_map/ppermute | solution.py:22
  94.9 3.6 %collective-permute-start.8 = (bf16[64,1024]{1,0:T(8,128)(2,1)S(1)}, bf16[64,1024]{1,0:T(8,128)(2,1)S(1)}, u32[]{:S(2)}, u32[]{:S(2)}) collective-permute-start(bf16[64,1024]{1,0:T(8,128)(2,1)S(1)} %collective-permute-done.7), channel_id=1, source_target_pairs={{1,0},{2,1},{3,2},{4,3},{5,4},{6,5},{7,6},{0,7},{9,8},{10,9},{11,1... | collective-permute-start | bytes 393224 | tf_op jit(solution)/shard_map/ppermute | solution.py:24
  98.5 2.7 %collective-permute-done.5 = bf16[64,1024]{1,0:T(8,128)(2,1)S(1)} collective-permute-done((bf16[64,1024]{1,0:T(8,128)(2,1)S(1)}, bf16[64,1024]{1,0:T(8,128)(2,1)S(1)}, u32[]{:S(2)}, u32[]{:S(2)}) %collective-permute-start.5) | collective-permute-done | bytes 131104 | tf_op jit(solution)/shard_map/ppermute | solution.py:22
  101.4 0.6 gather_fusion
  102.0 0.8 gather_fusion.1
  102.8 0.5 fusion.22
  103.3 0.2 copy_dynamic-update-slice_fusion.7
  103.5 1.8 %fusion.20 = f32[64,8,96]{2,0,1:T(8,128)S(1)} fusion(bf16[64,8,1024]{2,0,1:T(8,128)(2,1)} %copy-done.13, bf16[96,1024]{1,0:T(8,128)(2,1)S(1)} %gather_fusion.1, pred[96]{0:T(512)(128)(4,1)S(1)} %compare_and_fusion), kind=kOutput, calls=%fused_computation.59 | convolution fusion | flops 100761600 | bytes 1441888 | tf_op jit(solution)/shard_map/dot_general | solution.py:68
  105.4 0.5 fusion.18
  105.9 0.5 fusion.16
  106.4 0.5 fusion.14
  106.9 0.5 fusion.12
  107.4 0.5 fusion.10
  108.0 0.5 fusion.8
  108.5 0.2 copy_dynamic-update-slice_fusion.6
  108.6 0.2 copy_dynamic-update-slice_fusion.5
  108.8 0.2 copy_dynamic-update-slice_fusion.4
  109.0 0.2 copy_dynamic-update-slice_fusion.3
  109.1 0.2 copy_dynamic-update-slice_fusion.2
  109.3 0.2 copy_dynamic-update-slice_fusion.1
  109.5 0.2 copy_dynamic-update-slice_fusion
  109.6 1.2 %multiply_convert_fusion = bf16[64,64,96]{2,1,0:T(8,128)(2,1)} fusion(f32[64,64,96]{2,1,0:T(8,128)S(1)} %copy_dynamic-update-slice_fusion), kind=kLoop, calls=%fused_computation.4 | loop fusion | flops 786432 | bytes 2359296 | tf_op jit(solution)/shard_map/convert_element_type | solution.py:73
  (178 shorter events, 7.3 us)
Async XLA Ops:
  0.0 16.1 %copy-start = (bf16[64,1024]{1,0:T(8,128)(2,1)S(1)}, bf16[64,1024]{1,0:T(8,128)(2,1)}, u32[]{:S(2)}) copy-start(bf16[64,1024]{1,0:T(8,128)(2,1)} %param.4) | copy-start | bytes 393220
  16.1 9.3 %copy-start.14 = (f32[33]{0:T(128)S(1)}, f32[33]{0:T(128)}, u32[]{:S(2)}) copy-start(f32[33]{0:T(128)} %param.6) | copy-start | bytes 400
  16.1 10.8 %copy-start.16 = (u32[32]{0:T(128)S(1)}, u32[32]{0:T(128)}, u32[]{:S(2)}) copy-start(u32[32]{0:T(128)} %constant.175) | copy-start | bytes 388
  16.1 12.1 %copy-start.15 = (s32[1,12]{1,0:T(1,128)S(1)}, s32[1,12]{1,0:T(1,128)}, u32[]{:S(2)}) copy-start(s32[1,12]{1,0:T(1,128)} %param.7) | copy-start | bytes 148
  18.7 23.8 %collective-permute-start.1 = (bf16[16,1024]{1,0:T(8,128)(2,1)S(1)}, bf16[16,1024]{1,0:T(8,128)(2,1)S(1)}, u32[]{:S(2)}, u32[]{:S(2)}) collective-permute-start(bf16[16,1024]{1,0:T(8,128)(2,1)S(1)} %get-tuple-element.8), channel_id=1, source_target_pairs={{1,0},{2,1},{3,2},{4,3},{5,4},{6,5},{7,6},{8,7},{9,8},{10,9},{11,1... | collective-permute-start | bytes 98312 | tf_op jit(solution)/shard_map/ppermute | solution.py:39
  20.0 22.5 %collective-permute-start = (bf16[16,1024]{1,0:T(8,128)(2,1)S(1)}, bf16[16,1024]{1,0:T(8,128)(2,1)S(1)}, u32[]{:S(2)}, u32[]{:S(2)}) collective-permute-start(bf16[16,1024]{1,0:T(8,128)(2,1)S(1)} %get-tuple-element.7), channel_id=1, source_target_pairs={{0,1},{1,2},{2,3},{3,4},{4,5},{5,6},{6,7},{7,8},{8,9},{9,10},{10,1... | collective-permute-start | bytes 98312 | tf_op jit(solution)/shard_map/ppermute | solution.py:38
  65.2 12.7 %collective-permute-start.2 = (bf16[64,1024]{1,0:T(8,128)(2,1)S(1)}, bf16[64,1024]{1,0:T(8,128)(2,1)S(1)}, u32[]{:S(2)}, u32[]{:S(2)}) collective-permute-start(bf16[64,1024]{1,0:T(8,128)(2,1)S(1)} %get-tuple-element.6), channel_id=1, source_target_pairs={{0,1},{1,2},{2,3},{3,4},{4,5},{5,6},{6,7},{7,0},{8,9},{9,10},{10,1... | collective-permute-start | bytes 393224 | tf_op jit(solution)/shard_map/ppermute | solution.py:22
  67.3 18.7 %collective-permute-start.6 = (bf16[64,1024]{1,0:T(8,128)(2,1)S(1)}, bf16[64,1024]{1,0:T(8,128)(2,1)S(1)}, u32[]{:S(2)}, u32[]{:S(2)}) collective-permute-start(bf16[64,1024]{1,0:T(8,128)(2,1)S(1)} %get-tuple-element.6), channel_id=1, source_target_pairs={{1,0},{2,1},{3,2},{4,3},{5,4},{6,5},{7,6},{0,7},{9,8},{10,9},{11,1... | collective-permute-start | bytes 393224 | tf_op jit(solution)/shard_map/ppermute | solution.py:24
  75.8 1.0 copy-start.13
  76.0 1.2 %copy-start.11 = (bf16[64,8,1024]{2,0,1:T(8,128)(2,1)}, bf16[64,8,1024]{2,0,1:T(8,128)(2,1)S(1)}, u32[]{:S(2)}) copy-start(bf16[64,8,1024]{2,0,1:T(8,128)(2,1)S(1)} %constant_dynamic-update-slice_fusion.24) | copy-start | bytes 3145732
  76.2 1.3 %copy-start.9 = (bf16[64,8,1024]{2,0,1:T(8,128)(2,1)}, bf16[64,8,1024]{2,0,1:T(8,128)(2,1)S(1)}, u32[]{:S(2)}) copy-start(bf16[64,8,1024]{2,0,1:T(8,128)(2,1)S(1)} %constant_dynamic-update-slice_fusion.32) | copy-start | bytes 3145732
  76.9 1.0 copy-start.7
  77.3 8.5 %copy-start.5 = (bf16[64,8,1024]{2,0,1:T(8,128)(2,1)}, bf16[64,8,1024]{2,0,1:T(8,128)(2,1)S(1)}, u32[]{:S(2)}) copy-start(bf16[64,8,1024]{2,0,1:T(8,128)(2,1)S(1)} %constant_dynamic-update-slice_fusion.48) | copy-start | bytes 3145732
  77.6 23.7 %copy-start.3 = (bf16[64,8,1024]{2,0,1:T(8,128)(2,1)}, bf16[64,8,1024]{2,0,1:T(8,128)(2,1)S(1)}, u32[]{:S(2)}) copy-start(bf16[64,8,1024]{2,0,1:T(8,128)(2,1)S(1)} %constant_dynamic-update-slice_fusion.56) | copy-start | bytes 3145732
  77.9 7.8 %collective-permute-start.3 = (bf16[64,1024]{1,0:T(8,128)(2,1)S(1)}, bf16[64,1024]{1,0:T(8,128)(2,1)S(1)}, u32[]{:S(2)}, u32[]{:S(2)}) collective-permute-start(bf16[64,1024]{1,0:T(8,128)(2,1)S(1)} %collective-permute-done.2), channel_id=1, source_target_pairs={{0,1},{1,2},{2,3},{3,4},{4,5},{5,6},{6,7},{7,0},{8,9},{9,10},{10,1... | collective-permute-start | bytes 393224 | tf_op jit(solution)/shard_map/ppermute | solution.py:22
  85.7 7.8 %collective-permute-start.4 = (bf16[64,1024]{1,0:T(8,128)(2,1)S(1)}, bf16[64,1024]{1,0:T(8,128)(2,1)S(1)}, u32[]{:S(2)}, u32[]{:S(2)}) collective-permute-start(bf16[64,1024]{1,0:T(8,128)(2,1)S(1)} %collective-permute-done.3), channel_id=1, source_target_pairs={{0,1},{1,2},{2,3},{3,4},{4,5},{5,6},{6,7},{7,0},{8,9},{9,10},{10,1... | collective-permute-start | bytes 393224 | tf_op jit(solution)/shard_map/ppermute | solution.py:22
  85.9 8.9 %collective-permute-start.7 = (bf16[64,1024]{1,0:T(8,128)(2,1)S(1)}, bf16[64,1024]{1,0:T(8,128)(2,1)S(1)}, u32[]{:S(2)}, u32[]{:S(2)}) collective-permute-start(bf16[64,1024]{1,0:T(8,128)(2,1)S(1)} %collective-permute-done.6), channel_id=1, source_target_pairs={{1,0},{2,1},{3,2},{4,3},{5,4},{6,5},{7,6},{0,7},{9,8},{10,9},{11,1... | collective-permute-start | bytes 393224 | tf_op jit(solution)/shard_map/ppermute | solution.py:24
  93.4 7.8 %collective-permute-start.5 = (bf16[64,1024]{1,0:T(8,128)(2,1)S(1)}, bf16[64,1024]{1,0:T(8,128)(2,1)S(1)}, u32[]{:S(2)}, u32[]{:S(2)}) collective-permute-start(bf16[64,1024]{1,0:T(8,128)(2,1)S(1)} %collective-permute-done.4), channel_id=1, source_target_pairs={{0,1},{1,2},{2,3},{3,4},{4,5},{5,6},{6,7},{7,0},{8,9},{9,10},{10,1... | collective-permute-start | bytes 393224 | tf_op jit(solution)/shard_map/ppermute | solution.py:22
  94.9 6.5 %copy-start.1 = (bf16[64,8,1024]{2,0,1:T(8,128)(2,1)}, bf16[64,8,1024]{2,0,1:T(8,128)(2,1)S(1)}, u32[]{:S(2)}) copy-start(bf16[64,8,1024]{2,0,1:T(8,128)(2,1)S(1)} %constant_dynamic-update-slice_fusion.64) | copy-start | bytes 3145732
  94.9 6.5 %collective-permute-start.8 = (bf16[64,1024]{1,0:T(8,128)(2,1)S(1)}, bf16[64,1024]{1,0:T(8,128)(2,1)S(1)}, u32[]{:S(2)}, u32[]{:S(2)}) collective-permute-start(bf16[64,1024]{1,0:T(8,128)(2,1)S(1)} %collective-permute-done.7), channel_id=1, source_target_pairs={{1,0},{2,1},{3,2},{4,3},{5,4},{6,5},{7,6},{0,7},{9,8},{10,9},{11,1... | collective-permute-start | bytes 393224 | tf_op jit(solution)/shard_map/ppermute | solution.py:24
  102.8 2.5 %copy-start.12 = (bf16[64,8,1024]{2,0,1:T(8,128)(2,1)S(1)}, bf16[64,8,1024]{2,0,1:T(8,128)(2,1)}, u32[]{:S(2)}) copy-start(bf16[64,8,1024]{2,0,1:T(8,128)(2,1)} %copy-done.11) | copy-start | bytes 3145732
  103.3 2.6 %copy-start.10 = (bf16[64,8,1024]{2,0,1:T(8,128)(2,1)S(1)}, bf16[64,8,1024]{2,0,1:T(8,128)(2,1)}, u32[]{:S(2)}) copy-start(bf16[64,8,1024]{2,0,1:T(8,128)(2,1)} %copy-done.9) | copy-start | bytes 3145732
  103.5 2.9 %copy-start.8 = (bf16[64,8,1024]{2,0,1:T(8,128)(2,1)S(1)}, bf16[64,8,1024]{2,0,1:T(8,128)(2,1)}, u32[]{:S(2)}) copy-start(bf16[64,8,1024]{2,0,1:T(8,128)(2,1)} %copy-done.7) | copy-start | bytes 3145732
  105.3 1.6 %copy-start.6 = (bf16[64,8,1024]{2,0,1:T(8,128)(2,1)S(1)}, bf16[64,8,1024]{2,0,1:T(8,128)(2,1)}, u32[]{:S(2)}) copy-start(bf16[64,8,1024]{2,0,1:T(8,128)(2,1)} %copy-done.5) | copy-start | bytes 3145732
  105.9 1.6 %copy-start.4 = (bf16[64,8,1024]{2,0,1:T(8,128)(2,1)S(1)}, bf16[64,8,1024]{2,0,1:T(8,128)(2,1)}, u32[]{:S(2)}) copy-start(bf16[64,8,1024]{2,0,1:T(8,128)(2,1)} %copy-done.3) | copy-start | bytes 3145732
  106.4 1.6 %copy-start.2 = (bf16[64,8,1024]{2,0,1:T(8,128)(2,1)S(1)}, bf16[64,8,1024]{2,0,1:T(8,128)(2,1)}, u32[]{:S(2)}) copy-start(bf16[64,8,1024]{2,0,1:T(8,128)(2,1)} %copy-done.1) | copy-start | bytes 3145732
